TPU v7x, 128 devices: a whole 4x4x4 slice. The times are simulated.
128 devices in a mesh: vox: 8 (over y, core), fas: 16 (over z, x).
Axes of the slice: x: 4, y: 4, z: 4, core: 2. Of those that a mesh axis runs over, the one named last changes fastest.
Arguments:
- signal: float32 [128, 6144], P('vox', 'fas'), may hold values from -6 to 6
- initial_weights: float32 [524288], P('fas'), may hold values from 0.1 to 2
- coefficients: bfloat16 [32768, 4096], P(('vox', 'fas')), may hold values from 0 to 0.0234375
- block_rows: int32 [32768], P(('vox', 'fas')), may hold values from 0 to 127, as said below
- block_cols: int32 [32768], P(('vox', 'fas')), may hold values from 0 to 8191, as said below
- block_atoms: int32 [32768, 64], P(('vox', 'fas')), may hold values from 0 to 359
- block_count: int32 [128], P(('vox', 'fas')), may hold values from 64 to 256, as said below
- dictionary: bfloat16 [360, 96], replicated, may hold values from -6 to 6
Outputs:
- weights: float32 [524288], P('fas')
- residual: float32 [128, 6144], P('vox', 'fas')
Inputs may be any that keep to these rules, and one draw needn't show every extreme that they name: Block slots are stored device by device: the device with vox index i and fas index f holds slots (i * 16 + f) * 256 to (i * 16 + f + 1) * 256 - 1, and every block_rows value there lies in i * 16 to (i + 1) * 16 - 1. For the slots of the device with fas index f, every block_cols value lies in f * 512 to (f + 1) * 512 - 1. `block_count`: entry i * 16 + f is the number of live slots of the device with vox index i and fas index f, its first slots; some device has all 256 live.
All inputs are finite; a program needn't handle non-finite values.
Results may differ from a plain program's by a relative error of at most 0.0003.
Values sent between devices are 32-bit elements; how exact they have to be, the bound alone decides.
A program may use at most 128 MiB of HBM per device.

v0:
```python
import jax
import jax.numpy as jnp
from jax import lax
from jax.sharding import PartitionSpec as P

BV = 64
BF = 64
DIRS = 96
ITERS = 5


def local(
    signal,
    initial_weights,
    coefficients,
    block_rows,
    block_cols,
    block_atoms,
    block_count,
    dictionary,
):
    vox_rows = signal.shape[0]
    fas_rows = initial_weights.shape[0] // BF
    slot_total = coefficients.shape[0]
    row_width = BV * DIRS
    fas_place = lax.axis_index("fas")
    rows_local = block_rows - lax.axis_index("vox") * vox_rows
    cols_local = block_cols - fas_place * fas_rows
    live_count = block_count[0]
    atom_table = dictionary[block_atoms]
    coef_view = coefficients.reshape(slot_total, BV, BF)
    group_size = min(256, slot_total)
    group_turns = (live_count + group_size - 1) // group_size
    vox_range = jnp.arange(vox_rows, dtype=jnp.int32)
    fas_range = jnp.arange(fas_rows, dtype=jnp.int32)

    def group_pieces(first_slot):
        live_mask = (first_slot + jnp.arange(group_size, dtype=jnp.int32) < live_count).astype(
            jnp.float32
        )
        return (coef_view, atom_table, rows_local, cols_local, live_mask)

    def forward_partial(values):
        table = values.reshape(fas_rows, BF)

        def forward_accumulate(turn, running):
            coef_blk, atom_blk, rows_blk, cols_blk, live_mask = group_pieces(turn * group_size)
            scaled = coef_blk.astype(jnp.float32) * table[cols_blk][:, None, :]
            image_blk = jnp.einsum(
                "kvj,kjd->kvd",
                scaled,
                atom_blk.astype(jnp.float32),
                precision=lax.Precision.HIGHEST,
                preferred_element_type=jnp.float32,
            )
            selector = (rows_blk[:, None] == vox_range[None, :]).astype(jnp.float32) * live_mask[
                :, None
            ]
            added = jnp.dot(
                selector.T,
                image_blk.reshape(group_size, row_width),
                precision=lax.Precision.HIGHEST,
                preferred_element_type=jnp.float32,
            )
            return running + added

        start = jnp.zeros((vox_rows, row_width), jnp.float32)
        return lax.fori_loop(0, group_turns, forward_accumulate, start)

    def backward_partial(rows_view):

        def backward_accumulate(turn, running):
            coef_blk, atom_blk, rows_blk, cols_blk, live_mask = group_pieces(turn * group_size)
            gathered = rows_view[rows_blk]
            inner = jnp.einsum(
                "kvj,kvd->kjd",
                coef_blk.astype(jnp.float32),
                gathered,
                precision=lax.Precision.HIGHEST,
                preferred_element_type=jnp.float32,
            )
            contrib = jnp.sum(atom_blk.astype(jnp.float32) * inner, axis=-1)
            selector = (cols_blk[:, None] == fas_range[None, :]).astype(jnp.float32) * live_mask[
                :, None
            ]
            added = jnp.dot(
                selector.T,
                contrib,
                precision=lax.Precision.HIGHEST,
                preferred_element_type=jnp.float32,
            )
            return running + added

        start = jnp.zeros((fas_rows, BF), jnp.float32)
        running = lax.fori_loop(0, group_turns, backward_accumulate, start)
        return running.reshape(-1)

    def collect(partial_value):
        return lax.psum_scatter(partial_value, "fas", scatter_dimension=1, tiled=True)

    weights = initial_weights
    residual = collect(forward_partial(weights)) - signal
    for sweep in range(ITERS):
        whole_rows = lax.all_gather(residual, "fas", axis=1, tiled=True)
        gradient = lax.psum(backward_partial(whole_rows.reshape(vox_rows, BV, DIRS)), "vox")
        projected = jnp.where((weights > 0) | (gradient < 0), gradient, 0.0)
        image_pred = collect(forward_partial(projected))
        image_local = jnp.sum(image_pred * image_pred)
        grad_sq = lax.psum(jnp.sum(projected * projected), "fas")
        image_sq = lax.psum(image_local, ("vox", "fas"))
        step_size = grad_sq / (image_sq + 1e-06)
        weights = jnp.maximum(weights - step_size * projected, 0.0)
        residual = collect(forward_partial(weights)) - signal
    return (weights, residual)


def solution(mesh):
    placed = (
        P("vox", "fas"),
        P("fas"),
        P(("vox", "fas"), None),
        P(("vox", "fas")),
        P(("vox", "fas")),
        P(("vox", "fas"), None),
        P(("vox", "fas")),
        P(),
    )
    return jax.shard_map(
        local, mesh=mesh, in_specs=placed, out_specs=(P("fas"), P("vox", "fas")), check_vma=False
    )
```

profile of v0, /device:TPU:0, one launch (start us, length us, event | category | flops | bytes accessed | tf_op | source)
XLA Modules:
  0.0 2227.8 jit_solution(15539309578874618926)
XLA Ops:
  18.6 57.4 %gather_fusion = bf16[16384,96]{1,0:T(8,128)(2,1)} fusion(bf16[360,96]{1,0:T(8,128)(2,1)S(1)} %copy.28, s32[16384]{0:T(1024)S(1)} %broadcast_clamp_fusion), kind=kCustom, calls=%fused_computation | custom fusion | bytes 6356992 | tf_op jit(solution)/shard_map/gather | solution.py:30
  76.7 27.9 %while.208 = (s32[]{:T(128)}, f32[16,6144]{1,0:T(8,128)S(1)}, s32[]{:T(128)}, s32[256]{0:T(256)S(1)}, s32[]{:T(128)}, /*index=5*/bf16[256,64,64]{2,1,0:T(8,128)(...) while((s32[]{:T(128)}, f32[16,6144]{1,0:T(8,128)S(1)}, ...), condition=%wide.region_1.2_spmd.clone, body=%wide.region_0.1_spmd.clone.sunk | while | flops 1512153856 | bytes 31263864 | solution.py:68
  105.5 74.3 %reduce-scatter.12.cloned.1.call-done = f32[16,384]{1,0:T(8,128)} async-done(((f32[16,6144]{1,0:T(8,128)}), f32[16,384]{1,0:T(8,128)}) %reduce-scatter.12.cloned.1.call-update) | async-done | bytes 24592 | tf_op jit(solution)/shard_map/reduce_scatter | solution.py:99
  180.5 23.5 %all_gather.15 = f32[16,6144]{1,0:T(8,128)S(1)} all-gather(f32[16,384]{1,0:T(8,128)S(1)} %sub.58), channel_id=1, replica_groups=mesh['vox'=8,'fas'=16] {'fas'}, dimensions={1}, use_global_device_ids=true | all-gather | bytes 417792 | tf_op jit(solution)/shard_map/all_gather | solution.py:104
  208.6 13.4 fusion.156
  224.2 58.0 %all-reduce.6.cloned.1.call-done = f32[32768]{0:T(1024)} async-done(((f32[32768]{0:T(1024)}), f32[32768]{0:T(1024)}) %all-reduce.6.cloned.1.call-update) | async-done | bytes 131088 | tf_op jit(solution)/shard_map/psum | solution.py:105
  284.7 28.3 %while.210 = (s32[]{:T(128)}, f32[16,6144]{1,0:T(8,128)S(1)}, s32[]{:T(128)}, s32[256]{0:T(256)S(1)}, s32[]{:T(128)}, /*index=5*/bf16[256,64,64]{2,1,0:T(8,128)(...) while((s32[]{:T(128)}, f32[16,6144]{1,0:T(8,128)S(1)}, ...), condition=%wide.region_10.11_spmd.clone, body=%wide.region_9.10_spmd.clone.sunk | while | flops 1512153856 | bytes 31263864 | solution.py:68
  313.8 70.8 %reduce-scatter.14.cloned.1.call-done = f32[16,384]{1,0:T(8,128)} async-done(((f32[16,6144]{1,0:T(8,128)}), f32[16,384]{1,0:T(8,128)}) %reduce-scatter.14.cloned.1.call-update) | async-done | bytes 24592 | tf_op jit(solution)/shard_map/reduce_scatter | solution.py:99
  386.1 38.8 %psum.106 = f32[]{:T(128)} all-reduce(f32[]{:T(128)} %get-tuple-element.2460), channel_id=1, replica_groups=mesh['vox'=8,'fas'=16] {'fas'}, use_global_device_ids=true, to_apply=%region_8.9 | all-reduce | flops 1 | bytes 8 | tf_op jit(solution)/shard_map/psum | solution.py:109
  424.8 62.7 %psum.107 = f32[]{:T(128)} all-reduce(f32[]{:T(128)} %multiply_reduce_fusion.9), channel_id=1, replica_groups=mesh['vox'=8,'fas'=16] {'vox','fas'}, use_global_device_ids=true, to_apply=%region_13.14 | all-reduce | flops 1 | bytes 8 | tf_op jit(solution)/shard_map/psum | solution.py:110
  489.8 28.1 %while.211 = (s32[]{:T(128)}, f32[16,6144]{1,0:T(8,128)S(1)}, s32[]{:T(128)}, s32[256]{0:T(256)S(1)}, s32[]{:T(128)}, /*index=5*/bf16[256,64,64]{2,1,0:T(8,128)(...) while((s32[]{:T(128)}, f32[16,6144]{1,0:T(8,128)S(1)}, ...), condition=%wide.region_15.16_spmd.clone, body=%wide.region_14.15_spmd.clone.sunk | while | flops 1512153856 | bytes 31263864 | solution.py:68
  518.7 69.0 %reduce-scatter.16.cloned.1.call-done = f32[16,384]{1,0:T(8,128)} async-done(((f32[16,6144]{1,0:T(8,128)}), f32[16,384]{1,0:T(8,128)}) %reduce-scatter.16.cloned.1.call-update) | async-done | bytes 24592 | tf_op jit(solution)/shard_map/reduce_scatter | solution.py:99
  588.5 23.5 %all_gather.16 = f32[16,6144]{1,0:T(8,128)S(1)} all-gather(f32[16,384]{1,0:T(8,128)S(1)} %sub.60), channel_id=1, replica_groups=mesh['vox'=8,'fas'=16] {'fas'}, dimensions={1}, use_global_device_ids=true | all-gather | bytes 417792 | tf_op jit(solution)/shard_map/all_gather | solution.py:104
  616.6 13.4 fusion.157
  632.2 58.0 %all-reduce.8.cloned.1.call-done = f32[32768]{0:T(1024)} async-done(((f32[32768]{0:T(1024)}), f32[32768]{0:T(1024)}) %all-reduce.8.cloned.1.call-update) | async-done | bytes 131088 | tf_op jit(solution)/shard_map/psum | solution.py:105
  692.7 28.2 %while.213 = (s32[]{:T(128)}, f32[16,6144]{1,0:T(8,128)S(1)}, s32[]{:T(128)}, s32[256]{0:T(256)S(1)}, s32[]{:T(128)}, /*index=5*/bf16[256,64,64]{2,1,0:T(8,128)(...) while((s32[]{:T(128)}, f32[16,6144]{1,0:T(8,128)S(1)}, ...), condition=%wide.region_24.25_spmd.clone, body=%wide.region_23.24_spmd.clone.sunk | while | flops 1512153856 | bytes 31263864 | solution.py:68
  721.7 70.8 %reduce-scatter.18.cloned.1.call-done = f32[16,384]{1,0:T(8,128)} async-done(((f32[16,6144]{1,0:T(8,128)}), f32[16,384]{1,0:T(8,128)}) %reduce-scatter.18.cloned.1.call-update) | async-done | bytes 24592 | tf_op jit(solution)/shard_map/reduce_scatter | solution.py:99
  793.8 38.8 %psum.109 = f32[]{:T(128)} all-reduce(f32[]{:T(128)} %get-tuple-element.2458), channel_id=1, replica_groups=mesh['vox'=8,'fas'=16] {'fas'}, use_global_device_ids=true, to_apply=%region_22.23 | all-reduce | flops 1 | bytes 8 | tf_op jit(solution)/shard_map/psum | solution.py:109
  832.6 62.8 %psum.110 = f32[]{:T(128)} all-reduce(f32[]{:T(128)} %multiply_reduce_fusion.8), channel_id=1, replica_groups=mesh['vox'=8,'fas'=16] {'vox','fas'}, use_global_device_ids=true, to_apply=%region_27.28 | all-reduce | flops 1 | bytes 8 | tf_op jit(solution)/shard_map/psum | solution.py:110
  897.6 28.4 %while.214 = (s32[]{:T(128)}, f32[16,6144]{1,0:T(8,128)S(1)}, s32[]{:T(128)}, s32[256]{0:T(256)S(1)}, s32[]{:T(128)}, /*index=5*/bf16[256,64,64]{2,1,0:T(8,128)(...) while((s32[]{:T(128)}, f32[16,6144]{1,0:T(8,128)S(1)}, ...), condition=%wide.region_29.30_spmd.clone, body=%wide.region_28.29_spmd.clone.sunk | while | flops 1512153856 | bytes 31263864 | solution.py:68
  926.8 69.0 %reduce-scatter.20.cloned.1.call-done = f32[16,384]{1,0:T(8,128)} async-done(((f32[16,6144]{1,0:T(8,128)}), f32[16,384]{1,0:T(8,128)}) %reduce-scatter.20.cloned.1.call-update) | async-done | bytes 24592 | tf_op jit(solution)/shard_map/reduce_scatter | solution.py:99
  996.6 23.5 %all_gather.17 = f32[16,6144]{1,0:T(8,128)S(1)} all-gather(f32[16,384]{1,0:T(8,128)S(1)} %sub.62), channel_id=1, replica_groups=mesh['vox'=8,'fas'=16] {'fas'}, dimensions={1}, use_global_device_ids=true | all-gather | bytes 417792 | tf_op jit(solution)/shard_map/all_gather | solution.py:104
  1024.6 13.4 fusion.158
  1040.3 58.0 %all-reduce.10.cloned.1.call-done = f32[32768]{0:T(1024)} async-done(((f32[32768]{0:T(1024)}), f32[32768]{0:T(1024)}) %all-reduce.10.cloned.1.call-update) | async-done | bytes 131088 | tf_op jit(solution)/shard_map/psum | solution.py:105
  1100.7 28.1 %while.216 = (s32[]{:T(128)}, f32[16,6144]{1,0:T(8,128)S(1)}, s32[]{:T(128)}, s32[256]{0:T(256)S(1)}, s32[]{:T(128)}, /*index=5*/bf16[256,64,64]{2,1,0:T(8,128)(...) while((s32[]{:T(128)}, f32[16,6144]{1,0:T(8,128)S(1)}, ...), condition=%wide.region_38.39_spmd.clone, body=%wide.region_37.38_spmd.clone.sunk | while | flops 1512153856 | bytes 31263864 | solution.py:68
  1129.6 70.8 %reduce-scatter.22.cloned.1.call-done = f32[16,384]{1,0:T(8,128)} async-done(((f32[16,6144]{1,0:T(8,128)}), f32[16,384]{1,0:T(8,128)}) %reduce-scatter.22.cloned.1.call-update) | async-done | bytes 24592 | tf_op jit(solution)/shard_map/reduce_scatter | solution.py:99
  1201.9 38.8 %psum.112 = f32[]{:T(128)} all-reduce(f32[]{:T(128)} %get-tuple-element.2456), channel_id=1, replica_groups=mesh['vox'=8,'fas'=16] {'fas'}, use_global_device_ids=true, to_apply=%region_36.37 | all-reduce | flops 1 | bytes 8 | tf_op jit(solution)/shard_map/psum | solution.py:109
  1240.6 62.7 %psum.113 = f32[]{:T(128)} all-reduce(f32[]{:T(128)} %multiply_reduce_fusion.7), channel_id=1, replica_groups=mesh['vox'=8,'fas'=16] {'vox','fas'}, use_global_device_ids=true, to_apply=%region_41.42 | all-reduce | flops 1 | bytes 8 | tf_op jit(solution)/shard_map/psum | solution.py:110
  1305.6 28.3 %while.217 = (s32[]{:T(128)}, f32[16,6144]{1,0:T(8,128)S(1)}, s32[]{:T(128)}, s32[256]{0:T(256)S(1)}, s32[]{:T(128)}, /*index=5*/bf16[256,64,64]{2,1,0:T(8,128)(...) while((s32[]{:T(128)}, f32[16,6144]{1,0:T(8,128)S(1)}, ...), condition=%wide.region_43.44_spmd.clone, body=%wide.region_42.43_spmd.clone.sunk | while | flops 1512153856 | bytes 31263864 | solution.py:68
  1334.7 69.1 %reduce-scatter.24.cloned.1.call-done = f32[16,384]{1,0:T(8,128)} async-done(((f32[16,6144]{1,0:T(8,128)}), f32[16,384]{1,0:T(8,128)}) %reduce-scatter.24.cloned.1.call-update) | async-done | bytes 24592 | tf_op jit(solution)/shard_map/reduce_scatter | solution.py:99
  1404.5 23.5 %all_gather.18 = f32[16,6144]{1,0:T(8,128)S(1)} all-gather(f32[16,384]{1,0:T(8,128)S(1)} %sub.64), channel_id=1, replica_groups=mesh['vox'=8,'fas'=16] {'fas'}, dimensions={1}, use_global_device_ids=true | all-gather | bytes 417792 | tf_op jit(solution)/shard_map/all_gather | solution.py:104
  1432.6 13.4 fusion.159
  1448.3 57.9 %all-reduce.12.cloned.1.call-done = f32[32768]{0:T(1024)} async-done(((f32[32768]{0:T(1024)}), f32[32768]{0:T(1024)}) %all-reduce.12.cloned.1.call-update) | async-done | bytes 131088 | tf_op jit(solution)/shard_map/psum | solution.py:105
  1508.6 28.1 %while.219 = (s32[]{:T(128)}, f32[16,6144]{1,0:T(8,128)S(1)}, s32[]{:T(128)}, s32[256]{0:T(256)S(1)}, s32[]{:T(128)}, /*index=5*/bf16[256,64,64]{2,1,0:T(8,128)(...) while((s32[]{:T(128)}, f32[16,6144]{1,0:T(8,128)S(1)}, ...), condition=%wide.region_52.53_spmd.clone, body=%wide.region_51.52_spmd.clone.sunk | while | flops 1512153856 | bytes 31263864 | solution.py:68
  1537.6 70.8 %reduce-scatter.26.cloned.1.call-done = f32[16,384]{1,0:T(8,128)} async-done(((f32[16,6144]{1,0:T(8,128)}), f32[16,384]{1,0:T(8,128)}) %reduce-scatter.26.cloned.1.call-update) | async-done | bytes 24592 | tf_op jit(solution)/shard_map/reduce_scatter | solution.py:99
  1609.8 38.8 %psum.115 = f32[]{:T(128)} all-reduce(f32[]{:T(128)} %get-tuple-element.2454), channel_id=1, replica_groups=mesh['vox'=8,'fas'=16] {'fas'}, use_global_device_ids=true, to_apply=%region_50.51 | all-reduce | flops 1 | bytes 8 | tf_op jit(solution)/shard_map/psum | solution.py:109
  1648.6 62.8 %psum.116 = f32[]{:T(128)} all-reduce(f32[]{:T(128)} %multiply_reduce_fusion.6), channel_id=1, replica_groups=mesh['vox'=8,'fas'=16] {'vox','fas'}, use_global_device_ids=true, to_apply=%region_55.56 | all-reduce | flops 1 | bytes 8 | tf_op jit(solution)/shard_map/psum | solution.py:110
  1713.6 28.3 %while.220 = (s32[]{:T(128)}, f32[16,6144]{1,0:T(8,128)S(1)}, s32[]{:T(128)}, s32[256]{0:T(256)S(1)}, s32[]{:T(128)}, /*index=5*/bf16[256,64,64]{2,1,0:T(8,128)(...) while((s32[]{:T(128)}, f32[16,6144]{1,0:T(8,128)S(1)}, ...), condition=%wide.region_57.58_spmd.clone, body=%wide.region_56.57_spmd.clone.sunk | while | flops 1512153856 | bytes 31263864 | solution.py:68
  1742.7 69.0 %reduce-scatter.28.cloned.1.call-done = f32[16,384]{1,0:T(8,128)} async-done(((f32[16,6144]{1,0:T(8,128)}), f32[16,384]{1,0:T(8,128)}) %reduce-scatter.28.cloned.1.call-update) | async-done | bytes 24592 | tf_op jit(solution)/shard_map/reduce_scatter | solution.py:99
  1812.5 23.5 %all_gather.19 = f32[16,6144]{1,0:T(8,128)S(1)} all-gather(f32[16,384]{1,0:T(8,128)S(1)} %sub.66), channel_id=1, replica_groups=mesh['vox'=8,'fas'=16] {'fas'}, dimensions={1}, use_global_device_ids=true | all-gather | bytes 417792 | tf_op jit(solution)/shard_map/all_gather | solution.py:104
  1840.5 13.4 fusion.160
  1856.2 58.0 %all-reduce.14.cloned.1.call-done = f32[32768]{0:T(1024)} async-done(((f32[32768]{0:T(1024)}), f32[32768]{0:T(1024)}) %all-reduce.14.cloned.1.call-update) | async-done | bytes 131088 | tf_op jit(solution)/shard_map/psum | solution.py:105
  1916.6 28.1 %while.222 = (s32[]{:T(128)}, f32[16,6144]{1,0:T(8,128)S(1)}, s32[]{:T(128)}, s32[256]{0:T(256)S(1)}, s32[]{:T(128)}, /*index=5*/bf16[256,64,64]{2,1,0:T(8,128)(...) while((s32[]{:T(128)}, f32[16,6144]{1,0:T(8,128)S(1)}, ...), condition=%wide.region_66.67_spmd.clone, body=%wide.region_65.66_spmd.clone.sunk | while | flops 1512153856 | bytes 31263864 | solution.py:68
  1945.5 70.8 %reduce-scatter.30.cloned.1.call-done = f32[16,384]{1,0:T(8,128)} async-done(((f32[16,6144]{1,0:T(8,128)}), f32[16,384]{1,0:T(8,128)}) %reduce-scatter.30.cloned.1.call-update) | async-done | bytes 24592 | tf_op jit(solution)/shard_map/reduce_scatter | solution.py:99
  2017.8 38.8 %psum.118 = f32[]{:T(128)} all-reduce(f32[]{:T(128)} %get-tuple-element.2452), channel_id=1, replica_groups=mesh['vox'=8,'fas'=16] {'fas'}, use_global_device_ids=true, to_apply=%region_64.65 | all-reduce | flops 1 | bytes 8 | tf_op jit(solution)/shard_map/psum | solution.py:109
  2056.5 62.7 %psum.119 = f32[]{:T(128)} all-reduce(f32[]{:T(128)} %multiply_reduce_fusion.5), channel_id=1, replica_groups=mesh['vox'=8,'fas'=16] {'vox','fas'}, use_global_device_ids=true, to_apply=%region_69.70 | all-reduce | flops 1 | bytes 8 | tf_op jit(solution)/shard_map/psum | solution.py:110
  2121.5 28.2 %while.223 = (s32[]{:T(128)}, f32[16,6144]{1,0:T(8,128)S(1)}, s32[]{:T(128)}, s32[256]{0:T(256)S(1)}, s32[]{:T(128)}, /*index=5*/bf16[256,64,64]{2,1,0:T(8,128)(...) while((s32[]{:T(128)}, f32[16,6144]{1,0:T(8,128)S(1)}, ...), condition=%wide.region_71.72_spmd.clone, body=%wide.region_70.71_spmd.clone.sunk | while | flops 1512153856 | bytes 31263864 | solution.py:68
  2150.5 69.0 %reduce-scatter.32.cloned.1.call-done = f32[16,384]{1,0:T(8,128)} async-done(((f32[16,6144]{1,0:T(8,128)}), f32[16,384]{1,0:T(8,128)}) %reduce-scatter.32.cloned.1.call-update) | async-done | bytes 24592 | tf_op jit(solution)/shard_map/reduce_scatter | solution.py:99
  (217 shorter events, 395.2 us)
Async XLA Ops:
  7.2 10.8 copy-start.15
  7.2 11.1 copy-start.14
  7.2 11.2 copy-start.16
  7.2 11.2 copy-start.11
  7.2 172.5 %reduce-scatter.12.cloned.1.call-start = ((), (), s32[]{:S(2)}) async-start(), calls=%async_computation.11 | async-start | bytes 417792 | tf_op jit(solution)/shard_map/reduce_scatter | solution.py:99
  18.5 58.1 %copy-start.17 = (s32[256]{0:T(256)S(1)}, s32[256]{0:T(256)}, u32[]{:S(2)}) copy-start(s32[256]{0:T(256)} %param.43) | copy-start | bytes 3076
  76.7 103.0 %copy-start.12 = (f32[16,384]{1,0:T(8,128)S(1)}, f32[16,384]{1,0:T(8,128)}, u32[]{:S(2)}) copy-start(f32[16,384]{1,0:T(8,128)} %param.40) | copy-start | bytes 73732
  104.6 0.7 copy-start.1
  105.4 176.9 %all-reduce.6.cloned.1.call-start = ((), (), s32[]{:S(2)}) async-start(), calls=%async_computation.12 | async-start | bytes 262144 | tf_op jit(solution)/shard_map/psum | solution.py:105
  224.2 160.4 %reduce-scatter.14.cloned.1.call-start = ((), (), s32[]{:S(2)}) async-start(), calls=%async_computation.13 | async-start | bytes 417792 | tf_op jit(solution)/shard_map/reduce_scatter | solution.py:99
  313.0 0.7 copy-start.2
  313.8 274.0 %reduce-scatter.16.cloned.1.call-start = ((), (), s32[]{:S(2)}) async-start(), calls=%async_computation.14 | async-start | bytes 417792 | tf_op jit(solution)/shard_map/reduce_scatter | solution.py:99
  517.9 0.7 copy-start.3
  518.7 171.6 %all-reduce.8.cloned.1.call-start = ((), (), s32[]{:S(2)}) async-start(), calls=%async_computation.15 | async-start | bytes 262144 | tf_op jit(solution)/shard_map/psum | solution.py:105
  632.2 160.2 %reduce-scatter.18.cloned.1.call-start = ((), (), s32[]{:S(2)}) async-start(), calls=%async_computation.16 | async-start | bytes 417792 | tf_op jit(solution)/shard_map/reduce_scatter | solution.py:99
  720.8 0.7 copy-start.4
  721.6 274.2 %reduce-scatter.20.cloned.1.call-start = ((), (), s32[]{:S(2)}) async-start(), calls=%async_computation.17 | async-start | bytes 417792 | tf_op jit(solution)/shard_map/reduce_scatter | solution.py:99
  926.0 0.7 copy-start.5
  926.8 171.5 %all-reduce.10.cloned.1.call-start = ((), (), s32[]{:S(2)}) async-start(), calls=%async_computation.18 | async-start | bytes 262144 | tf_op jit(solution)/shard_map/psum | solution.py:105
  1040.2 160.2 %reduce-scatter.22.cloned.1.call-start = ((), (), s32[]{:S(2)}) async-start(), calls=%async_computation.19 | async-start | bytes 417792 | tf_op jit(solution)/shard_map/reduce_scatter | solution.py:99
  1128.8 0.7 copy-start.6
  1129.6 274.2 %reduce-scatter.24.cloned.1.call-start = ((), (), s32[]{:S(2)}) async-start(), calls=%async_computation.20 | async-start | bytes 417792 | tf_op jit(solution)/shard_map/reduce_scatter | solution.py:99
  1333.9 0.7 copy-start.7
  1334.7 171.5 %all-reduce.12.cloned.1.call-start = ((), (), s32[]{:S(2)}) async-start(), calls=%async_computation.21 | async-start | bytes 262144 | tf_op jit(solution)/shard_map/psum | solution.py:105
  1448.2 160.2 %reduce-scatter.26.cloned.1.call-start = ((), (), s32[]{:S(2)}) async-start(), calls=%async_computation.22 | async-start | bytes 417792 | tf_op jit(solution)/shard_map/reduce_scatter | solution.py:99
  1536.8 0.7 copy-start.8
  1537.5 274.2 %reduce-scatter.28.cloned.1.call-start = ((), (), s32[]{:S(2)}) async-start(), calls=%async_computation.23 | async-start | bytes 417792 | tf_op jit(solution)/shard_map/reduce_scatter | solution.py:99
  1741.9 0.7 copy-start.9
  1742.7 171.5 %all-reduce.14.cloned.1.call-start = ((), (), s32[]{:S(2)}) async-start(), calls=%async_computation.24 | async-start | bytes 262144 | tf_op jit(solution)/shard_map/psum | solution.py:105
  1856.1 160.2 %reduce-scatter.30.cloned.1.call-start = ((), (), s32[]{:S(2)}) async-start(), calls=%async_computation.25 | async-start | bytes 417792 | tf_op jit(solution)/shard_map/reduce_scatter | solution.py:99
  1944.7 0.7 copy-start.10
  1945.5 274.0 %reduce-scatter.32.cloned.1.call-start = ((), (), s32[]{:S(2)}) async-start(), calls=%async_computation.26 | async-start | bytes 417792 | tf_op jit(solution)/shard_map/reduce_scatter | solution.py:99
  2120.6 0.9 copy-start.13
  2149.7 0.7 copy-start
Sparse Core Ops, SparseCore 0:
  105.5 74.1 reduce-scatter.11
  224.3 57.9 all-reduce.5
  313.9 70.6 reduce-scatter.13
  518.8 68.9 reduce-scatter.15
  632.3 57.8 all-reduce.7
  721.7 70.6 reduce-scatter.17
  926.9 68.9 reduce-scatter.19
  1040.4 57.8 all-reduce.9
  1129.7 70.6 reduce-scatter.21
  1334.8 68.9 reduce-scatter.23
  1448.3 57.8 all-reduce.11
  1537.7 70.6 reduce-scatter.25
  1742.8 68.9 reduce-scatter.27
  1856.3 57.8 all-reduce.13
  1945.6 70.6 reduce-scatter.29
  2150.6 68.8 reduce-scatter.31
where the time goes:
time: 2240 us; the launch traced here: 2230 us
  waiting for transfers between devices  1060 us (47%)
  blocking collectives  625 us (28%)
  matrix products  275 us (12%)
  local copies, waits for them, and re-layouts  207 us (9%)
  other arithmetic  30.5 us (1%)
  between operations  22.5 us (1%)
    reduce_scatter x11, waiting for transfers between devices, collect(): lax.psum_scatter(partial_value, 'fas', scatter_dimension=1, tiled=True)  773 us
    psum x5, blocking collectives, local(): image_sq = lax.psum(image_local, ('vox', 'fas'))  314 us
    psum x5, waiting for transfers between devices, local(): lax.psum(backward_partial(whole_rows.reshape(vox_rows, BV, DIRS)), 'vox')  290 us
    psum x5, blocking collectives, local(): grad_sq = lax.psum(jnp.sum(projected * projected), 'fas')  194 us
    dot_general x11, matrix products, forward_accumulate(): jnp.einsum('kvj,kjd->kvd', scaled, atom_blk.astype(jnp.float32), precisio...  124 us
    all_gather x5, blocking collectives, local(): whole_rows = lax.all_gather(residual, 'fas', axis=1, tiled=True)  118 us
    dot_general x11, local copies, waits for them, and re-layouts, forward_accumulate(): jnp.einsum('kvj,kjd->kvd', scaled, atom_blk.astype(jnp.float32), precisio...  94.4 us
    dot_general x11, matrix products, forward_accumulate(): jnp.dot(selector.T, image_blk.reshape(group_size, row_width), precision=l...  81.8 us
  transfers between devices with their start and end apart: 16, of which 16 were waited for; matrix products, arithmetic and copies ran while one was open for 0% of the time, Pallas kernels for 0%

commit v1 on v0

--- a/solution.py
+++ b/solution.py
@@ -102,7 +102,9 @@
     residual = collect(forward_partial(weights)) - signal
     for sweep in range(ITERS):
         whole_rows = lax.all_gather(residual, "fas", axis=1, tiled=True)
-        gradient = lax.psum(backward_partial(whole_rows.reshape(vox_rows, BV, DIRS)), "vox")
+        part = backward_partial(whole_rows.reshape(vox_rows, BV, DIRS))
+        pieces = lax.all_gather(part, "vox", axis=0, tiled=False)
+        gradient = pieces.sum(axis=0)
         projected = jnp.where((weights > 0) | (gradient < 0), gradient, 0.0)
         image_pred = collect(forward_partial(projected))
         image_local = jnp.sum(image_pred * image_pred)

time: 2240 us -> 2070 us (0.924)
  waiting for transfers between devices: 1060 us -> 888 us
    psum x5 -> x0, waiting for transfers between devices: 290 us -> none  [local(): lax.psum(backward_partial(whole_rows.reshape(vox_rows, BV, DIRS)), 'vox')]
    all_gather x0 -> x5, waiting for transfers between devices: none -> 110 us  [local(): pieces = lax.all_gather(part, 'vox', axis=0, tiled=False)]
where the time goes in v1:
time: 2070 us; the launch traced here: 2060 us
  waiting for transfers between devices  888 us (43%)
  blocking collectives  626 us (30%)
  matrix products  275 us (13%)
  local copies, waits for them, and re-layouts  207 us (10%)
  other arithmetic  35.9 us (2%)
  between operations  22.3 us (1%)
    reduce_scatter x11, waiting for transfers between devices, collect(): lax.psum_scatter(partial_value, 'fas', scatter_dimension=1, tiled=True)  777 us
    psum x5, blocking collectives, local(): image_sq = lax.psum(image_local, ('vox', 'fas'))  314 us
    psum x5, blocking collectives, local(): grad_sq = lax.psum(jnp.sum(projected * projected), 'fas')  194 us
    dot_general x11, matrix products, forward_accumulate(): jnp.einsum('kvj,kjd->kvd', scaled, atom_blk.astype(jnp.float32), precisio...  124 us
    all_gather x5, blocking collectives, local(): whole_rows = lax.all_gather(residual, 'fas', axis=1, tiled=True)  119 us
    all_gather x5, waiting for transfers between devices, local(): pieces = lax.all_gather(part, 'vox', axis=0, tiled=False)  110 us
    dot_general x11, local copies, waits for them, and re-layouts, forward_accumulate(): jnp.einsum('kvj,kjd->kvd', scaled, atom_blk.astype(jnp.float32), precisio...  94.4 us
    dot_general x11, matrix products, forward_accumulate(): jnp.dot(selector.T, image_blk.reshape(group_size, row_width), precision=l...  81.8 us
  transfers between devices with their start and end apart: 16, of which 16 were waited for; matrix products, arithmetic and copies ran while one was open for 0% of the time, Pallas kernels for 0%

profile of v1, /device:TPU:0, one launch (start us, length us, event | category | flops | bytes accessed | tf_op | source)
XLA Modules:
  0.0 2058.1 jit_solution(8206460509092669613)
XLA Ops:
  18.6 57.4 %gather_fusion = bf16[16384,96]{1,0:T(8,128)(2,1)} fusion(bf16[360,96]{1,0:T(8,128)(2,1)S(1)} %copy.63, s32[16384]{0:T(1024)S(1)} %broadcast_clamp_fusion), kind=kCustom, calls=%fused_computation | custom fusion | bytes 6356992 | tf_op jit(solution)/shard_map/gather | solution.py:30
  76.7 27.9 %while.208 = (s32[]{:T(128)}, f32[16,6144]{1,0:T(8,128)S(1)}, s32[]{:T(128)}, s32[256]{0:T(256)S(1)}, s32[]{:T(128)}, /*index=5*/bf16[256,64,64]{2,1,0:T(8,128)(...) while((s32[]{:T(128)}, f32[16,6144]{1,0:T(8,128)S(1)}, ...), condition=%wide.region_1.2_spmd.clone, body=%wide.region_0.1_spmd.clone.sunk | while | flops 1512153856 | bytes 31263864 | solution.py:68
  105.5 74.3 %reduce-scatter.12.cloned.1.call-done = f32[16,384]{1,0:T(8,128)} async-done(((f32[16,6144]{1,0:T(8,128)}), f32[16,384]{1,0:T(8,128)}) %reduce-scatter.12.cloned.1.call-update) | async-done | bytes 24592 | tf_op jit(solution)/shard_map/reduce_scatter | solution.py:99
  180.5 23.8 %all_gather.30 = f32[16,6144]{1,0:T(8,128)S(1)} all-gather(f32[16,384]{1,0:T(8,128)S(1)} %sub.58), channel_id=1, replica_groups=mesh['vox'=8,'fas'=16] {'fas'}, dimensions={1}, use_global_device_ids=true | all-gather | bytes 417792 | tf_op jit(solution)/shard_map/all_gather | solution.py:104
  208.8 13.4 fusion.156
  224.6 22.1 %all-gather.11.cloned.1.call-done = f32[8,1,32768]{2,1,0:T(1,128)} async-done(((f32[1,1,32768]{2,1,0:T(1,128)}), f32[8,1,32768]{2,1,0:T(1,128)}) %all-gather.11.cloned.1.call-update) | async-done | bytes 1048592 | tf_op jit(solution)/shard_map/all_gather | solution.py:106
  250.2 28.1 %while.210 = (s32[]{:T(128)}, f32[16,6144]{1,0:T(8,128)S(1)}, s32[]{:T(128)}, s32[256]{0:T(256)S(1)}, s32[]{:T(128)}, /*index=5*/bf16[256,64,64]{2,1,0:T(8,128)(...) while((s32[]{:T(128)}, f32[16,6144]{1,0:T(8,128)S(1)}, ...), condition=%wide.region_10.11_spmd.clone, body=%wide.region_9.10_spmd.clone.sunk | while | flops 1512153856 | bytes 31263864 | solution.py:68
  279.1 71.6 %reduce-scatter.14.cloned.1.call-done = f32[16,384]{1,0:T(8,128)} async-done(((f32[16,6144]{1,0:T(8,128)}), f32[16,384]{1,0:T(8,128)}) %reduce-scatter.14.cloned.1.call-update) | async-done | bytes 24592 | tf_op jit(solution)/shard_map/reduce_scatter | solution.py:99
  352.1 38.8 %psum.70 = f32[]{:T(128)} all-reduce(f32[]{:T(128)} %get-tuple-element.2548), channel_id=1, replica_groups=mesh['vox'=8,'fas'=16] {'fas'}, use_global_device_ids=true, to_apply=%region_8.9 | all-reduce | flops 1 | bytes 8 | tf_op jit(solution)/shard_map/psum | solution.py:111
  390.9 62.7 %psum.71 = f32[]{:T(128)} all-reduce(f32[]{:T(128)} %multiply_reduce_fusion.9), channel_id=1, replica_groups=mesh['vox'=8,'fas'=16] {'vox','fas'}, use_global_device_ids=true, to_apply=%region_13.14 | all-reduce | flops 1 | bytes 8 | tf_op jit(solution)/shard_map/psum | solution.py:112
  455.9 28.1 %while.211 = (s32[]{:T(128)}, f32[16,6144]{1,0:T(8,128)S(1)}, s32[]{:T(128)}, s32[256]{0:T(256)S(1)}, s32[]{:T(128)}, /*index=5*/bf16[256,64,64]{2,1,0:T(8,128)(...) while((s32[]{:T(128)}, f32[16,6144]{1,0:T(8,128)S(1)}, ...), condition=%wide.region_15.16_spmd.clone, body=%wide.region_14.15_spmd.clone.sunk | while | flops 1512153856 | bytes 31263864 | solution.py:68
  484.8 69.0 %reduce-scatter.16.cloned.1.call-done = f32[16,384]{1,0:T(8,128)} async-done(((f32[16,6144]{1,0:T(8,128)}), f32[16,384]{1,0:T(8,128)}) %reduce-scatter.16.cloned.1.call-update) | async-done | bytes 24592 | tf_op jit(solution)/shard_map/reduce_scatter | solution.py:99
  554.6 23.8 %all_gather.32 = f32[16,6144]{1,0:T(8,128)S(1)} all-gather(f32[16,384]{1,0:T(8,128)S(1)} %sub.60), channel_id=1, replica_groups=mesh['vox'=8,'fas'=16] {'fas'}, dimensions={1}, use_global_device_ids=true | all-gather | bytes 417792 | tf_op jit(solution)/shard_map/all_gather | solution.py:104
  582.9 13.4 fusion.157
  598.6 22.1 %all-gather.13.cloned.1.call-done = f32[8,1,32768]{2,1,0:T(1,128)} async-done(((f32[1,1,32768]{2,1,0:T(1,128)}), f32[8,1,32768]{2,1,0:T(1,128)}) %all-gather.13.cloned.1.call-update) | async-done | bytes 1048592 | tf_op jit(solution)/shard_map/all_gather | solution.py:106
  624.2 28.1 %while.213 = (s32[]{:T(128)}, f32[16,6144]{1,0:T(8,128)S(1)}, s32[]{:T(128)}, s32[256]{0:T(256)S(1)}, s32[]{:T(128)}, /*index=5*/bf16[256,64,64]{2,1,0:T(8,128)(...) while((s32[]{:T(128)}, f32[16,6144]{1,0:T(8,128)S(1)}, ...), condition=%wide.region_24.25_spmd.clone, body=%wide.region_23.24_spmd.clone.sunk | while | flops 1512153856 | bytes 31263864 | solution.py:68
  653.1 71.6 %reduce-scatter.18.cloned.1.call-done = f32[16,384]{1,0:T(8,128)} async-done(((f32[16,6144]{1,0:T(8,128)}), f32[16,384]{1,0:T(8,128)}) %reduce-scatter.18.cloned.1.call-update) | async-done | bytes 24592 | tf_op jit(solution)/shard_map/reduce_scatter | solution.py:99
  726.1 38.8 %psum.72 = f32[]{:T(128)} all-reduce(f32[]{:T(128)} %get-tuple-element.2546), channel_id=1, replica_groups=mesh['vox'=8,'fas'=16] {'fas'}, use_global_device_ids=true, to_apply=%region_22.23 | all-reduce | flops 1 | bytes 8 | tf_op jit(solution)/shard_map/psum | solution.py:111
  764.9 62.7 %psum.73 = f32[]{:T(128)} all-reduce(f32[]{:T(128)} %multiply_reduce_fusion.8), channel_id=1, replica_groups=mesh['vox'=8,'fas'=16] {'vox','fas'}, use_global_device_ids=true, to_apply=%region_27.28 | all-reduce | flops 1 | bytes 8 | tf_op jit(solution)/shard_map/psum | solution.py:112
  829.9 28.1 %while.214 = (s32[]{:T(128)}, f32[16,6144]{1,0:T(8,128)S(1)}, s32[]{:T(128)}, s32[256]{0:T(256)S(1)}, s32[]{:T(128)}, /*index=5*/bf16[256,64,64]{2,1,0:T(8,128)(...) while((s32[]{:T(128)}, f32[16,6144]{1,0:T(8,128)S(1)}, ...), condition=%wide.region_29.30_spmd.clone, body=%wide.region_28.29_spmd.clone.sunk | while | flops 1512153856 | bytes 31263864 | solution.py:68
  858.9 69.0 %reduce-scatter.20.cloned.1.call-done = f32[16,384]{1,0:T(8,128)} async-done(((f32[16,6144]{1,0:T(8,128)}), f32[16,384]{1,0:T(8,128)}) %reduce-scatter.20.cloned.1.call-update) | async-done | bytes 24592 | tf_op jit(solution)/shard_map/reduce_scatter | solution.py:99
  928.6 23.7 %all_gather.34 = f32[16,6144]{1,0:T(8,128)S(1)} all-gather(f32[16,384]{1,0:T(8,128)S(1)} %sub.62), channel_id=1, replica_groups=mesh['vox'=8,'fas'=16] {'fas'}, dimensions={1}, use_global_device_ids=true | all-gather | bytes 417792 | tf_op jit(solution)/shard_map/all_gather | solution.py:104
  956.9 13.4 fusion.158
  972.6 22.1 %all-gather.15.cloned.1.call-done = f32[8,1,32768]{2,1,0:T(1,128)} async-done(((f32[1,1,32768]{2,1,0:T(1,128)}), f32[8,1,32768]{2,1,0:T(1,128)}) %all-gather.15.cloned.1.call-update) | async-done | bytes 1048592 | tf_op jit(solution)/shard_map/all_gather | solution.py:106
  998.2 28.1 %while.216 = (s32[]{:T(128)}, f32[16,6144]{1,0:T(8,128)S(1)}, s32[]{:T(128)}, s32[256]{0:T(256)S(1)}, s32[]{:T(128)}, /*index=5*/bf16[256,64,64]{2,1,0:T(8,128)(...) while((s32[]{:T(128)}, f32[16,6144]{1,0:T(8,128)S(1)}, ...), condition=%wide.region_38.39_spmd.clone, body=%wide.region_37.38_spmd.clone.sunk | while | flops 1512153856 | bytes 31263864 | solution.py:68
  1027.1 71.6 %reduce-scatter.22.cloned.1.call-done = f32[16,384]{1,0:T(8,128)} async-done(((f32[16,6144]{1,0:T(8,128)}), f32[16,384]{1,0:T(8,128)}) %reduce-scatter.22.cloned.1.call-update) | async-done | bytes 24592 | tf_op jit(solution)/shard_map/reduce_scatter | solution.py:99
  1100.2 38.8 %psum.74 = f32[]{:T(128)} all-reduce(f32[]{:T(128)} %get-tuple-element.2544), channel_id=1, replica_groups=mesh['vox'=8,'fas'=16] {'fas'}, use_global_device_ids=true, to_apply=%region_36.37 | all-reduce | flops 1 | bytes 8 | tf_op jit(solution)/shard_map/psum | solution.py:111
  1138.9 62.7 %psum.75 = f32[]{:T(128)} all-reduce(f32[]{:T(128)} %multiply_reduce_fusion.7), channel_id=1, replica_groups=mesh['vox'=8,'fas'=16] {'vox','fas'}, use_global_device_ids=true, to_apply=%region_41.42 | all-reduce | flops 1 | bytes 8 | tf_op jit(solution)/shard_map/psum | solution.py:112
  1203.9 28.1 %while.217 = (s32[]{:T(128)}, f32[16,6144]{1,0:T(8,128)S(1)}, s32[]{:T(128)}, s32[256]{0:T(256)S(1)}, s32[]{:T(128)}, /*index=5*/bf16[256,64,64]{2,1,0:T(8,128)(...) while((s32[]{:T(128)}, f32[16,6144]{1,0:T(8,128)S(1)}, ...), condition=%wide.region_43.44_spmd.clone, body=%wide.region_42.43_spmd.clone.sunk | while | flops 1512153856 | bytes 31263864 | solution.py:68
  1232.9 69.0 %reduce-scatter.24.cloned.1.call-done = f32[16,384]{1,0:T(8,128)} async-done(((f32[16,6144]{1,0:T(8,128)}), f32[16,384]{1,0:T(8,128)}) %reduce-scatter.24.cloned.1.call-update) | async-done | bytes 24592 | tf_op jit(solution)/shard_map/reduce_scatter | solution.py:99
  1302.7 23.7 %all_gather.36 = f32[16,6144]{1,0:T(8,128)S(1)} all-gather(f32[16,384]{1,0:T(8,128)S(1)} %sub.64), channel_id=1, replica_groups=mesh['vox'=8,'fas'=16] {'fas'}, dimensions={1}, use_global_device_ids=true | all-gather | bytes 417792 | tf_op jit(solution)/shard_map/all_gather | solution.py:104
  1331.0 13.4 fusion.159
  1346.7 22.1 %all-gather.17.cloned.1.call-done = f32[8,1,32768]{2,1,0:T(1,128)} async-done(((f32[1,1,32768]{2,1,0:T(1,128)}), f32[8,1,32768]{2,1,0:T(1,128)}) %all-gather.17.cloned.1.call-update) | async-done | bytes 1048592 | tf_op jit(solution)/shard_map/all_gather | solution.py:106
  1372.3 28.1 %while.219 = (s32[]{:T(128)}, f32[16,6144]{1,0:T(8,128)S(1)}, s32[]{:T(128)}, s32[256]{0:T(256)S(1)}, s32[]{:T(128)}, /*index=5*/bf16[256,64,64]{2,1,0:T(8,128)(...) while((s32[]{:T(128)}, f32[16,6144]{1,0:T(8,128)S(1)}, ...), condition=%wide.region_52.53_spmd.clone, body=%wide.region_51.52_spmd.clone.sunk | while | flops 1512153856 | bytes 31263864 | solution.py:68
  1401.2 71.6 %reduce-scatter.26.cloned.1.call-done = f32[16,384]{1,0:T(8,128)} async-done(((f32[16,6144]{1,0:T(8,128)}), f32[16,384]{1,0:T(8,128)}) %reduce-scatter.26.cloned.1.call-update) | async-done | bytes 24592 | tf_op jit(solution)/shard_map/reduce_scatter | solution.py:99
  1474.2 38.8 %psum.76 = f32[]{:T(128)} all-reduce(f32[]{:T(128)} %get-tuple-element.2542), channel_id=1, replica_groups=mesh['vox'=8,'fas'=16] {'fas'}, use_global_device_ids=true, to_apply=%region_50.51 | all-reduce | flops 1 | bytes 8 | tf_op jit(solution)/shard_map/psum | solution.py:111
  1513.0 62.7 %psum.77 = f32[]{:T(128)} all-reduce(f32[]{:T(128)} %multiply_reduce_fusion.6), channel_id=1, replica_groups=mesh['vox'=8,'fas'=16] {'vox','fas'}, use_global_device_ids=true, to_apply=%region_55.56 | all-reduce | flops 1 | bytes 8 | tf_op jit(solution)/shard_map/psum | solution.py:112
  1578.0 28.1 %while.220 = (s32[]{:T(128)}, f32[16,6144]{1,0:T(8,128)S(1)}, s32[]{:T(128)}, s32[256]{0:T(256)S(1)}, s32[]{:T(128)}, /*index=5*/bf16[256,64,64]{2,1,0:T(8,128)(...) while((s32[]{:T(128)}, f32[16,6144]{1,0:T(8,128)S(1)}, ...), condition=%wide.region_57.58_spmd.clone, body=%wide.region_56.57_spmd.clone.sunk | while | flops 1512153856 | bytes 31263864 | solution.py:68
  1606.9 69.0 %reduce-scatter.28.cloned.1.call-done = f32[16,384]{1,0:T(8,128)} async-done(((f32[16,6144]{1,0:T(8,128)}), f32[16,384]{1,0:T(8,128)}) %reduce-scatter.28.cloned.1.call-update) | async-done | bytes 24592 | tf_op jit(solution)/shard_map/reduce_scatter | solution.py:99
  1676.6 23.8 %all_gather.38 = f32[16,6144]{1,0:T(8,128)S(1)} all-gather(f32[16,384]{1,0:T(8,128)S(1)} %sub.66), channel_id=1, replica_groups=mesh['vox'=8,'fas'=16] {'fas'}, dimensions={1}, use_global_device_ids=true | all-gather | bytes 417792 | tf_op jit(solution)/shard_map/all_gather | solution.py:104
  1704.9 13.4 fusion.160
  1720.7 22.1 %all-gather.19.cloned.1.call-done = f32[8,1,32768]{2,1,0:T(1,128)} async-done(((f32[1,1,32768]{2,1,0:T(1,128)}), f32[8,1,32768]{2,1,0:T(1,128)}) %all-gather.19.cloned.1.call-update) | async-done | bytes 1048592 | tf_op jit(solution)/shard_map/all_gather | solution.py:106
  1746.3 28.1 %while.222 = (s32[]{:T(128)}, f32[16,6144]{1,0:T(8,128)S(1)}, s32[]{:T(128)}, s32[256]{0:T(256)S(1)}, s32[]{:T(128)}, /*index=5*/bf16[256,64,64]{2,1,0:T(8,128)(...) while((s32[]{:T(128)}, f32[16,6144]{1,0:T(8,128)S(1)}, ...), condition=%wide.region_66.67_spmd.clone, body=%wide.region_65.66_spmd.clone.sunk | while | flops 1512153856 | bytes 31263864 | solution.py:68
  1775.2 71.6 %reduce-scatter.30.cloned.1.call-done = f32[16,384]{1,0:T(8,128)} async-done(((f32[16,6144]{1,0:T(8,128)}), f32[16,384]{1,0:T(8,128)}) %reduce-scatter.30.cloned.1.call-update) | async-done | bytes 24592 | tf_op jit(solution)/shard_map/reduce_scatter | solution.py:99
  1848.2 38.8 %psum.78 = f32[]{:T(128)} all-reduce(f32[]{:T(128)} %get-tuple-element.2540), channel_id=1, replica_groups=mesh['vox'=8,'fas'=16] {'fas'}, use_global_device_ids=true, to_apply=%region_64.65 | all-reduce | flops 1 | bytes 8 | tf_op jit(solution)/shard_map/psum | solution.py:111
  1887.0 62.8 %psum.79 = f32[]{:T(128)} all-reduce(f32[]{:T(128)} %multiply_reduce_fusion.5), channel_id=1, replica_groups=mesh['vox'=8,'fas'=16] {'vox','fas'}, use_global_device_ids=true, to_apply=%region_69.70 | all-reduce | flops 1 | bytes 8 | tf_op jit(solution)/shard_map/psum | solution.py:112
  1952.0 28.1 %while.223 = (s32[]{:T(128)}, f32[16,6144]{1,0:T(8,128)S(1)}, s32[]{:T(128)}, s32[256]{0:T(256)S(1)}, s32[]{:T(128)}, /*index=5*/bf16[256,64,64]{2,1,0:T(8,128)(...) while((s32[]{:T(128)}, f32[16,6144]{1,0:T(8,128)S(1)}, ...), condition=%wide.region_71.72_spmd.clone, body=%wide.region_70.71_spmd.clone.sunk | while | flops 1512153856 | bytes 31263864 | solution.py:68
  1980.9 69.1 %reduce-scatter.32.cloned.1.call-done = f32[16,384]{1,0:T(8,128)} async-done(((f32[16,6144]{1,0:T(8,128)}), f32[16,384]{1,0:T(8,128)}) %reduce-scatter.32.cloned.1.call-update) | async-done | bytes 24592 | tf_op jit(solution)/shard_map/reduce_scatter | solution.py:99
  (222 shorter events, 401.0 us)
Async XLA Ops:
  7.2 10.8 copy-start.15
  7.2 11.1 copy-start.14
  7.2 11.2 copy-start.16
  7.2 11.2 copy-start.11
  7.2 172.5 %reduce-scatter.12.cloned.1.call-start = ((), (), s32[]{:S(2)}) async-start(), calls=%async_computation.11 | async-start | bytes 417792 | tf_op jit(solution)/shard_map/reduce_scatter | solution.py:99
  18.5 58.1 %copy-start.17 = (s32[256]{0:T(256)S(1)}, s32[256]{0:T(256)}, u32[]{:S(2)}) copy-start(s32[256]{0:T(256)} %param.43) | copy-start | bytes 3076
  76.7 103.0 %copy-start.12 = (f32[16,384]{1,0:T(8,128)S(1)}, f32[16,384]{1,0:T(8,128)}, u32[]{:S(2)}) copy-start(f32[16,384]{1,0:T(8,128)} %param.40) | copy-start | bytes 73732
  104.6 0.7 copy-start.1
  105.4 141.2 %all-gather.11.cloned.1.call-start = ((), (), s32[]{:S(2)}) async-start(), calls=%async_computation.22 | async-start | bytes 1179648 | tf_op jit(solution)/shard_map/all_gather | solution.py:106
  224.5 126.1 %reduce-scatter.14.cloned.1.call-start = ((), (), s32[]{:S(2)}) async-start(), calls=%async_computation.12 | async-start | bytes 417792 | tf_op jit(solution)/shard_map/reduce_scatter | solution.py:99
  278.3 0.7 copy-start.2
  279.1 274.8 %reduce-scatter.16.cloned.1.call-start = ((), (), s32[]{:S(2)}) async-start(), calls=%async_computation.13 | async-start | bytes 417792 | tf_op jit(solution)/shard_map/reduce_scatter | solution.py:99
  484.0 0.7 copy-start.3
  484.8 135.9 %all-gather.13.cloned.1.call-start = ((), (), s32[]{:S(2)}) async-start(), calls=%async_computation.23 | async-start | bytes 1179648 | tf_op jit(solution)/shard_map/all_gather | solution.py:106
  598.6 126.1 %reduce-scatter.18.cloned.1.call-start = ((), (), s32[]{:S(2)}) async-start(), calls=%async_computation.14 | async-start | bytes 417792 | tf_op jit(solution)/shard_map/reduce_scatter | solution.py:99
  652.3 0.7 copy-start.4
  653.1 274.8 %reduce-scatter.20.cloned.1.call-start = ((), (), s32[]{:S(2)}) async-start(), calls=%async_computation.15 | async-start | bytes 417792 | tf_op jit(solution)/shard_map/reduce_scatter | solution.py:99
  858.0 0.7 copy-start.5
  858.8 135.9 %all-gather.15.cloned.1.call-start = ((), (), s32[]{:S(2)}) async-start(), calls=%async_computation.24 | async-start | bytes 1179648 | tf_op jit(solution)/shard_map/all_gather | solution.py:106
  972.6 126.2 %reduce-scatter.22.cloned.1.call-start = ((), (), s32[]{:S(2)}) async-start(), calls=%async_computation.16 | async-start | bytes 417792 | tf_op jit(solution)/shard_map/reduce_scatter | solution.py:99
  1026.3 0.7 copy-start.6
  1027.1 274.8 %reduce-scatter.24.cloned.1.call-start = ((), (), s32[]{:S(2)}) async-start(), calls=%async_computation.17 | async-start | bytes 417792 | tf_op jit(solution)/shard_map/reduce_scatter | solution.py:99
  1232.1 0.7 copy-start.7
  1232.8 135.9 %all-gather.17.cloned.1.call-start = ((), (), s32[]{:S(2)}) async-start(), calls=%async_computation.25 | async-start | bytes 1179648 | tf_op jit(solution)/shard_map/all_gather | solution.py:106
  1346.7 126.1 %reduce-scatter.26.cloned.1.call-start = ((), (), s32[]{:S(2)}) async-start(), calls=%async_computation.18 | async-start | bytes 417792 | tf_op jit(solution)/shard_map/reduce_scatter | solution.py:99
  1400.4 0.7 copy-start.8
  1401.2 274.7 %reduce-scatter.28.cloned.1.call-start = ((), (), s32[]{:S(2)}) async-start(), calls=%async_computation.19 | async-start | bytes 417792 | tf_op jit(solution)/shard_map/reduce_scatter | solution.py:99
  1606.1 0.7 copy-start.9
  1606.9 135.9 %all-gather.19.cloned.1.call-start = ((), (), s32[]{:S(2)}) async-start(), calls=%async_computation.26 | async-start | bytes 1179648 | tf_op jit(solution)/shard_map/all_gather | solution.py:106
  1720.6 126.2 %reduce-scatter.30.cloned.1.call-start = ((), (), s32[]{:S(2)}) async-start(), calls=%async_computation.20 | async-start | bytes 417792 | tf_op jit(solution)/shard_map/reduce_scatter | solution.py:99
  1774.3 0.7 copy-start.10
  1775.1 274.9 %reduce-scatter.32.cloned.1.call-start = ((), (), s32[]{:S(2)}) async-start(), calls=%async_computation.21 | async-start | bytes 417792 | tf_op jit(solution)/shard_map/reduce_scatter | solution.py:99
  1951.1 0.9 copy-start.13
  1980.1 0.7 copy-start
Sparse Core Ops, SparseCore 0:
  105.5 74.1 reduce-scatter.11
  224.7 21.9 all-gather.10
  279.2 71.4 reduce-scatter.13
  484.9 68.9 reduce-scatter.15
  598.7 21.9 all-gather.12
  653.2 71.4 reduce-scatter.17
  858.9 68.9 reduce-scatter.19
  972.7 21.9 all-gather.14
  1027.2 71.5 reduce-scatter.21
  1233.0 68.9 reduce-scatter.23
  1346.8 21.9 all-gather.16
  1401.3 71.4 reduce-scatter.25
  1607.0 68.8 reduce-scatter.27
  1720.8 21.9 all-gather.18
  1775.2 71.5 reduce-scatter.29
  1981.0 68.9 reduce-scatter.31
